TPU v7x, 128 devices: a whole 4x4x4 slice. The times are simulated.
128 devices in a mesh: img: 4 (over z_lo, core), exp: 32 (over x, y, z_hi).
Axes of the slice: x: 4, y: 4, z: 4 (z_hi: 2, z_lo: 2; z = z_hi * 2 + z_lo), core: 2. Of those that a mesh axis runs over, the one named last changes fastest.
Arguments:
- context: bfloat16 [256, 256, 1024], P(('img', 'exp')), may hold values from -1.5 to 1.5
- residual: bfloat16 [256, 256, 1024], P(('img', 'exp')), may hold values from -1.5 to 1.5
- cotangent: bfloat16 [256, 256, 1024], P(('img', 'exp')), may hold values from -6 to 6
- proj_weight: bfloat16 [1024, 1024], P('img'), may hold values from -0.1875 to 0.1875
- slot_params: bfloat16 [1024, 64], replicated, may hold values from -0.1875 to 0.1875
- expert_in: bfloat16 [64, 1024, 4096], P('exp', None, 'img'), may hold values from -0.1875 to 0.1875
- expert_out: bfloat16 [64, 4096, 1024], P('exp', 'img'), may hold values from -0.09375 to 0.09375
Outputs:
- grad_context: bfloat16 [256, 256, 1024], P(('img', 'exp'))
- grad_residual: bfloat16 [256, 256, 1024], P(('img', 'exp'))
- grad_proj: float32 [1024, 1024], P('img')
- grad_slots: float32 [1024, 64], replicated
- grad_expert_in: bfloat16 [64, 1024, 4096], P('exp', None, 'img')
- grad_expert_out: bfloat16 [64, 4096, 1024], P('exp', 'img')
All inputs are finite; a program needn't handle non-finite values.
Results may differ from a plain program's by a relative error of at most 0.025.
Values may be sent and summed in bfloat16 or wider, within the bound.
A program may use at most 128 MiB of HBM per device.

v0:
```python
import math
import jax
import jax.numpy as jnp
from jax import lax
from jax.sharding import Mesh
from jax.sharding import PartitionSpec as P

IMG = ("img_0", "img_1")
IMG_EXP = ("img_0", "img_1", "exp")
logit_scale = 48.0
epsilon = 1e-06


def copy_for_each(shard, axis):
    devices = lax.axis_size(axis)
    return lax.all_to_all(
        jnp.broadcast_to(shard[None], (devices, *shard.shape)), axis, 0, 0, tiled=True
    )


def laid_out(pieces, dim):
    pieces = jnp.moveaxis(pieces, 0, dim)
    dims = pieces.shape
    return pieces.reshape(*dims[:dim], dims[dim] * dims[dim + 1], *dims[dim + 2 :])


def gather_directly(shard, axis, dim):
    pieces = copy_for_each(shard, axis)
    return laid_out(pieces, dim)


def split_up(shard, dim, devices):
    before, after = (shard.shape[:dim], shard.shape[dim + 1 :])
    return jnp.moveaxis(shard.reshape(*before, devices, -1, *after), dim, 0)


def summed_on_arrival(shard, axis, dim):
    devices = lax.axis_size(axis)
    pieces = lax.all_to_all(split_up(shard, dim, devices), axis, 0, 0, tiled=True)
    return jnp.sum(pieces.astype(jnp.float32), axis=0)


def sum_in_two_steps(shard, axes, dim):
    far, near = axes
    own = summed_on_arrival(split_up(shard, dim, lax.axis_size(far)), near, dim + 1)
    return jnp.sum(
        lax.all_to_all(own.astype(jnp.bfloat16), far, 0, 0, tiled=True).astype(jnp.float32), axis=0
    )


def padded_to(lines, devices):
    spare = -lines.shape[0] % devices
    if not spare:
        return lines
    return jnp.concatenate([lines, jnp.zeros((spare, *lines.shape[1:]), lines.dtype)])


def nested_sum(shard, axes):
    lines = shard.reshape(-1, shard.shape[-1])
    own = summed_on_arrival(padded_to(lines, lax.axis_size(axes)), axes, 0)
    whole = gather_directly(own.astype(jnp.bfloat16), axes, 0)
    return whole[: len(lines)].reshape(shard.shape).astype(jnp.float32)


def gelu_back(pre, upstream):
    return jax.vjp(jax.nn.gelu, pre)[1](upstream)[0]


def shards(context, residual, cotangent, proj_weight, slot_params, expert_in, expert_out):
    images, tokens, width = context.shape
    rows = images * tokens
    factor = logit_scale / math.sqrt(width)
    flat_ctx = context.reshape(rows, width)
    columns = flat_ctx
    mixed = jnp.dot(
        columns, gather_directly(proj_weight, IMG, 0), preferred_element_type=jnp.float32
    )
    stream = (residual.reshape(rows, width).astype(jnp.float32) + mixed).astype(jnp.bfloat16)
    stream32 = stream.astype(jnp.float32)
    inverse = lax.rsqrt(jnp.mean(stream32 * stream32, axis=-1, keepdims=True) + epsilon)
    normed32 = stream32 * inverse
    normed = normed32.astype(jnp.bfloat16)
    params32 = slot_params.astype(jnp.float32)
    slot_norm = jnp.sqrt(jnp.sum(params32 * params32, axis=0, keepdims=True) + epsilon)
    unit32 = params32 / slot_norm
    unit = unit32.astype(jnp.bfloat16)
    logits = factor * jnp.dot(normed, unit, preferred_element_type=jnp.float32)
    logits = logits.reshape(images, tokens, -1)
    expo = jnp.exp(logits)
    dispatch32 = expo / jnp.sum(expo, axis=1, keepdims=True)
    combine32 = expo / jnp.sum(expo, axis=2, keepdims=True)
    dispatch = dispatch32.astype(jnp.bfloat16)
    combine = combine32.astype(jnp.bfloat16)
    normed3 = normed.reshape(images, tokens, width)
    slot_in = jnp.einsum(
        "bms,bmd->bsd", dispatch, normed3, preferred_element_type=jnp.float32
    ).astype(jnp.bfloat16)
    sent = lax.all_to_all(slot_in, "exp", split_axis=1, concat_axis=0, tiled=True)
    slot_rows = gather_directly(sent, IMG, 0)
    pre = jnp.einsum("gjd,jdf->gjf", slot_rows, expert_in, preferred_element_type=jnp.float32)
    act = jax.nn.gelu(pre).astype(jnp.bfloat16)
    piece = act
    summed = summed_on_arrival(
        jnp.einsum("gjf,jfd->gjd", piece, expert_out, preferred_element_type=jnp.float32).astype(
            jnp.bfloat16
        ),
        IMG,
        0,
    )
    slot_out = lax.all_to_all(
        summed.astype(jnp.bfloat16), "exp", split_axis=0, concat_axis=1, tiled=True
    )
    grad_slot_out = jnp.einsum(
        "bms,bmd->bsd", combine, cotangent, preferred_element_type=jnp.float32
    ).astype(jnp.bfloat16)
    grad_sent = lax.all_to_all(grad_slot_out, "exp", split_axis=1, concat_axis=0, tiled=True)
    grad_gathered = gather_directly(grad_sent, IMG, 0)
    grad_combine = jnp.einsum(
        "bmd,bsd->bms", cotangent, slot_out, preferred_element_type=jnp.float32
    )
    grad_act = jnp.einsum(
        "gjd,jfd->gjf", grad_gathered, expert_out, preferred_element_type=jnp.float32
    )
    grad_pre = gelu_back(pre, grad_act).astype(jnp.bfloat16)
    grad_expert_out = jnp.einsum(
        "gjf,gjd->jfd", act, grad_gathered, preferred_element_type=jnp.float32
    ).astype(jnp.bfloat16)
    grad_expert_in = jnp.einsum(
        "gjd,gjf->jdf", slot_rows, grad_pre, preferred_element_type=jnp.float32
    ).astype(jnp.bfloat16)
    piece = grad_pre
    grad_summed = summed_on_arrival(
        jnp.einsum("gjf,jdf->gjd", piece, expert_in, preferred_element_type=jnp.float32).astype(
            jnp.bfloat16
        ),
        IMG,
        0,
    )
    grad_slot_in = lax.all_to_all(
        grad_summed.astype(jnp.bfloat16), "exp", split_axis=0, concat_axis=1, tiled=True
    )
    grad_dispatch = jnp.einsum(
        "bmd,bsd->bms", normed3, grad_slot_in, preferred_element_type=jnp.float32
    )
    grad_logits32 = combine32 * (
        grad_combine - jnp.sum(combine32 * grad_combine, axis=2, keepdims=True)
    )
    grad_logits32 = grad_logits32 + dispatch32 * (
        grad_dispatch - jnp.sum(dispatch32 * grad_dispatch, axis=1, keepdims=True)
    )
    grad_logits = grad_logits32.astype(jnp.bfloat16).reshape(rows, -1)
    grad_normed = jnp.einsum(
        "bms,bsd->bmd", dispatch, grad_slot_in, preferred_element_type=jnp.float32
    ).reshape(rows, width)
    grad_normed = grad_normed + factor * jnp.dot(
        grad_logits, unit.T, preferred_element_type=jnp.float32
    )
    local_unit = factor * jnp.dot(normed.T, grad_logits, preferred_element_type=jnp.float32)
    grad_unit = lax.psum(local_unit, IMG_EXP)
    grad_slots = (
        grad_unit - unit32 * jnp.sum(unit32 * grad_unit, axis=0, keepdims=True)
    ) / slot_norm
    upstream = cotangent.reshape(rows, width).astype(jnp.float32)
    grad_stream = upstream + inverse * (
        grad_normed - normed32 * jnp.mean(normed32 * grad_normed, axis=-1, keepdims=True)
    )
    grad_residual = grad_stream.astype(jnp.bfloat16)
    grad_context = jnp.dot(
        grad_residual, gather_directly(proj_weight, IMG, 0).T, preferred_element_type=jnp.float32
    ).astype(jnp.bfloat16)
    columns = flat_ctx
    owned = sum_in_two_steps(
        jnp.dot(columns.T, grad_residual, preferred_element_type=jnp.float32).astype(jnp.bfloat16),
        ("img_0", "img_1"),
        0,
    )
    grad_proj = nested_sum(owned.astype(jnp.bfloat16), "exp")
    return (
        grad_context.reshape(images, tokens, width),
        grad_residual.reshape(images, tokens, width),
        grad_proj,
        grad_slots,
        grad_expert_in,
        grad_expert_out,
    )


def solution(mesh):
    torus = Mesh(mesh.devices.reshape(2, 2, mesh.shape["exp"]), ("img_0", "img_1", "exp"))
    placed = (
        P(IMG_EXP, None, None),
        P(IMG_EXP, None, None),
        P(IMG_EXP, None, None),
        P(IMG, None),
        P(),
        P("exp", None, IMG),
        P("exp", IMG, None),
    )
    return jax.shard_map(
        shards,
        mesh=torus,
        in_specs=placed,
        out_specs=(
            P(IMG_EXP, None, None),
            P(IMG_EXP, None, None),
            P(IMG, None),
            P(),
            P("exp", None, IMG),
            P("exp", IMG, None),
        ),
        check_vma=False,
    )
```

profile of v0, /device:TPU:1, one launch (start us, length us, event | category | flops | bytes accessed | tf_op | source)
XLA Modules:
  0.0 417.2 jit_solution(16925801770048762867)
XLA Ops:
  7.2 2.7 broadcast_in_dim.12
  9.9 5.1 %all-to-all-start = ((bf16[4,256,1024]{2,1,0:T(8,128)(2,1)}), bf16[4,256,1024]{2,1,0:T(8,128)(2,1)S(1)}, u32[]{:S(2)}, u32[]{:S(2)}) async-start(bf16[4,256,1024]{2,1,0:T(8,128)(2,1)} %broadcast_in_dim.12), calls=%async_computation | async-start | bytes 4194304 | tf_op jit(solution)/shard_map/all_to_all | solution.py:16
  15.1 24.5 %all-to-all-done = bf16[4,256,1024]{2,1,0:T(8,128)(2,1)S(1)} async-done(((bf16[4,256,1024]{2,1,0:T(8,128)(2,1)}), bf16[4,256,1024]{2,1,0:T(8,128)(2,1)S(1)}, u32[]{:S(2)}, u32[]{:S(2)}) %all-to-all-start) | async-done | bytes 2097184 | tf_op jit(solution)/shard_map/all_to_all | solution.py:16
  41.0 3.2 fusion.10
  48.0 10.6 %all-to-all-start.3 = ((bf16[2,64,1024]{2,0,1:T(2,128)(2,1)}), bf16[2,64,1024]{2,0,1:T(2,128)(2,1)}, u32[]{:S(2)}, u32[]{:S(2)}) async-start(bf16[2,64,1024]{2,0,1:T(2,128)(2,1)} %copy.81), calls=%async_computation.3 | async-start | bytes 524288 | tf_op jit(solution)/shard_map/all_to_all | solution.py:98
  61.2 7.1 %all-to-all-done.3 = bf16[2,64,1024]{2,0,1:T(2,128)(2,1)} async-done(((bf16[2,64,1024]{2,0,1:T(2,128)(2,1)}), bf16[2,64,1024]{2,0,1:T(2,128)(2,1)}, u32[]{:S(2)}, u32[]{:S(2)}) %all-to-all-start.3) | async-done | bytes 262176 | tf_op jit(solution)/shard_map/all_to_all | solution.py:98
  68.2 4.6 %all-to-all-start.1 = ((bf16[2,64,1024]{2,0,1:T(2,128)(2,1)}), bf16[2,64,1024]{2,0,1:T(2,128)(2,1)}, u32[]{:S(2)}, u32[]{:S(2)}) async-start(bf16[2,64,1024]{2,0,1:T(2,128)(2,1)} %copy.77), calls=%async_computation.1 | async-start | bytes 524288 | tf_op jit(solution)/shard_map/all_to_all | solution.py:116
  74.7 7.6 %all-to-all-done.1 = bf16[2,64,1024]{2,0,1:T(2,128)(2,1)} async-done(((bf16[2,64,1024]{2,0,1:T(2,128)(2,1)}), bf16[2,64,1024]{2,0,1:T(2,128)(2,1)}, u32[]{:S(2)}, u32[]{:S(2)}) %all-to-all-start.1) | async-done | bytes 262176 | tf_op jit(solution)/shard_map/all_to_all | solution.py:116
  82.3 2.0 broadcast_in_dim.16
  84.4 7.7 %all-to-all-start.4 = ((bf16[4,64,2,1024]{3,1,2,0:T(8,128)(2,1)}), bf16[4,64,2,1024]{3,1,2,0:T(8,128)(2,1)}, u32[]{:S(2)}, u32[]{:S(2)}) async-start(bf16[4,64,2,1024]{3,1,2,0:T(8,128)(2,1)} %broadcast_in_dim.16), calls=%async_computation.4 | async-start | bytes 2097152 | tf_op jit(solution)/shard_map/all_to_all | solution.py:16
  93.9 11.7 %all-to-all-done.4 = bf16[4,64,2,1024]{3,1,2,0:T(8,128)(2,1)} async-done(((bf16[4,64,2,1024]{3,1,2,0:T(8,128)(2,1)}), bf16[4,64,2,1024]{3,1,2,0:T(8,128)(2,1)}, u32[]{:S(2)}, u32[]{:S(2)}) %all-to-all-start.4) | async-done | bytes 1048608 | tf_op jit(solution)/shard_map/all_to_all | solution.py:16
  105.6 2.0 broadcast_in_dim.14
  107.6 5.2 %all-to-all-start.2 = ((bf16[4,64,2,1024]{3,1,2,0:T(8,128)(2,1)}), bf16[4,64,2,1024]{3,1,2,0:T(8,128)(2,1)}, u32[]{:S(2)}, u32[]{:S(2)}) async-start(bf16[4,64,2,1024]{3,1,2,0:T(8,128)(2,1)} %broadcast_in_dim.14), calls=%async_computation.2 | async-start | bytes 2097152 | tf_op jit(solution)/shard_map/all_to_all | solution.py:16
  115.1 4.8 %fusion.45 = f32[2,256,1024]{2,1,0:T(8,128)} fusion(bf16[256,2,1024]{2,0,1:T(8,128)(2,1)S(1)} %bitcast.141, bf16[2,1024,1024]{2,1,0:T(8,128)(2,1)} %param.12), kind=kOutput, calls=%fused_computation.75 | convolution fusion | flops 1073741824 | bytes 7340032 | tf_op jit(solution)/shard_map/gjd,jdf->gjf/dot_general | solution.py:100
  119.9 6.5 %all-to-all-done.2 = bf16[4,64,2,1024]{3,1,2,0:T(8,128)(2,1)} async-done(((bf16[4,64,2,1024]{3,1,2,0:T(8,128)(2,1)}), bf16[4,64,2,1024]{3,1,2,0:T(8,128)(2,1)}, u32[]{:S(2)}, u32[]{:S(2)}) %all-to-all-start.2) | async-done | bytes 1048608 | tf_op jit(solution)/shard_map/all_to_all | solution.py:16
  128.3 4.7 %fusion.17 = bf16[256,2,1024]{2,0,1:T(8,128)(2,1)S(1)} fusion(f32[2,256,1024]{2,1,0:T(8,128)S(1)} %copy-done.5, bf16[256,2,1024]{2,0,1:T(8,128)(2,1)S(1)} %bitcast.153, bf16[2,1024,1024]{2,1,0:T(8,128)(2,1)} %param.13), kind=kOutput, calls=%fused_computation.23 | convolution fusion | flops 1084227584 | bytes 8388608 | tf_op jit(solution)/shard_map/gjd,jfd->gjf/dot_general | solution.py:121
  135.5 5.2 %all-to-all-start.5 = ((bf16[4,64,2,1024]{3,1,2,0:T(8,128)(2,1)}), bf16[4,64,2,1024]{3,1,2,0:T(8,128)(2,1)}, u32[]{:S(2)}, u32[]{:S(2)}) async-start(bf16[4,64,2,1024]{3,1,2,0:T(8,128)(2,1)} %copy.85), calls=%async_computation.5 | async-start | bytes 2097152 | tf_op jit(solution)/shard_map/all_to_all | solution.py:39
  140.6 4.2 %convolution_convert_fusion.4 = bf16[2,256,1024]{2,1,0:T(8,128)(2,1)S(1)} fusion(bf16[2,1024,1024]{2,1,0:T(8,128)(2,1)} %param.13, f32[2,256,1024]{2,1,0:T(8,128)} %fusion.45), kind=kOutput, calls=%fused_computation.37 | convolution fusion | flops 1078984704 | bytes 7340032 | tf_op jit(solution)/shard_map/gjf,jfd->gjd/dot_general | solution.py:104
  146.0 8.2 %all-to-all-done.5 = bf16[4,64,2,1024]{3,1,2,0:T(8,128)(2,1)} async-done(((bf16[4,64,2,1024]{3,1,2,0:T(8,128)(2,1)}), bf16[4,64,2,1024]{3,1,2,0:T(8,128)(2,1)}, u32[]{:S(2)}, u32[]{:S(2)}) %all-to-all-start.5) | async-done | bytes 1048608 | tf_op jit(solution)/shard_map/all_to_all | solution.py:39
  154.2 5.2 %all-to-all-start.7 = ((bf16[4,64,2,1024]{3,1,2,0:T(8,128)(2,1)}), bf16[4,64,2,1024]{3,1,2,0:T(8,128)(2,1)}, u32[]{:S(2)}, u32[]{:S(2)}) async-start(bf16[4,64,2,1024]{3,1,2,0:T(8,128)(2,1)} %copy.89), calls=%async_computation.7 | async-start | bytes 2097152 | tf_op jit(solution)/shard_map/all_to_all | solution.py:39
  159.4 2.2 reduce_sum.136
  161.6 1.9 copy.87
  163.5 9.5 %all-to-all-done.7 = bf16[4,64,2,1024]{3,1,2,0:T(8,128)(2,1)} async-done(((bf16[4,64,2,1024]{3,1,2,0:T(8,128)(2,1)}), bf16[4,64,2,1024]{3,1,2,0:T(8,128)(2,1)}, u32[]{:S(2)}, u32[]{:S(2)}) %all-to-all-start.7) | async-done | bytes 1048608 | tf_op jit(solution)/shard_map/all_to_all | solution.py:39
  173.0 4.6 %all-to-all-start.6 = ((bf16[64,2,1024]{2,1,0:T(2,128)(2,1)}), bf16[64,2,1024]{2,1,0:T(2,128)(2,1)}, u32[]{:S(2)}, u32[]{:S(2)}) async-start(bf16[64,2,1024]{2,1,0:T(2,128)(2,1)} %copy.87), calls=%async_computation.6 | async-start | bytes 524288 | tf_op jit(solution)/shard_map/all_to_all | solution.py:139
  177.6 2.2 reduce_sum.137
  179.8 1.9 copy.91
  181.7 5.5 %all-to-all-done.6 = bf16[64,2,1024]{2,1,0:T(2,128)(2,1)} async-done(((bf16[64,2,1024]{2,1,0:T(2,128)(2,1)}), bf16[64,2,1024]{2,1,0:T(2,128)(2,1)}, u32[]{:S(2)}, u32[]{:S(2)}) %all-to-all-start.6) | async-done | bytes 262176 | tf_op jit(solution)/shard_map/all_to_all | solution.py:139
  187.2 4.6 %all-to-all-start.8 = ((bf16[64,2,1024]{2,1,0:T(2,128)(2,1)}), bf16[64,2,1024]{2,1,0:T(2,128)(2,1)}, u32[]{:S(2)}, u32[]{:S(2)}) async-start(bf16[64,2,1024]{2,1,0:T(2,128)(2,1)} %copy.91), calls=%async_computation.8 | async-start | bytes 524288 | tf_op jit(solution)/shard_map/all_to_all | solution.py:110
  191.8 1.8 copy.88
  195.4 5.9 %all-to-all-done.8 = bf16[64,2,1024]{2,1,0:T(2,128)(2,1)} async-done(((bf16[64,2,1024]{2,1,0:T(2,128)(2,1)}), bf16[64,2,1024]{2,1,0:T(2,128)(2,1)}, u32[]{:S(2)}, u32[]{:S(2)}) %all-to-all-start.8) | async-done | bytes 262176 | tf_op jit(solution)/shard_map/all_to_all | solution.py:110
  201.3 1.8 copy.92
  204.9 1.8 convolution_bitcast_fusion
  207.4 1.9 fusion.37
  209.2 1.9 fusion.30
  211.1 2.4 fusion.5
  215.7 9.3 %all_to_all.112 = bf16[2,2,256,1024]{3,2,1,0:T(8,128)(2,1)} all-to-all(bf16[2,2,256,1024]{3,2,1,0:T(8,128)(2,1)S(1)} %bitcast.143), channel_id=1, replica_groups=mesh['img_0'=2,'img_1'=2,'exp'=32] {'img_1'}, dimensions={0} | all-to-all | bytes 4194304 | tf_op jit(solution)/shard_map/all_to_all | solution.py:39
  225.0 3.4 reduce_sum.141
  228.4 4.4 %all-to-all-start.10 = ((bf16[2,256,1024]{2,1,0:T(8,128)(2,1)}), bf16[2,256,1024]{2,1,0:T(8,128)(2,1)}, u32[]{:S(2)}, u32[]{:S(2)}) async-start(bf16[2,256,1024]{2,1,0:T(8,128)(2,1)} %reduce_sum.141), calls=%async_computation.10 | async-start | bytes 2097152 | tf_op jit(solution)/shard_map/all_to_all | solution.py:47
  232.8 5.1 %convolution_convert_fusion = bf16[2,1024,1024]{2,1,0:T(8,128)(2,1)} fusion(bf16[256,2,1024]{2,0,1:T(8,128)(2,1)S(1)} %bitcast.154, f32[2,256,1024]{2,1,0:T(8,128)} %fusion.45), kind=kOutput, calls=%fused_computation.4 | convolution fusion | flops 1080557568 | bytes 7340032 | tf_op jit(solution)/shard_map/gjf,gjd->jfd/dot_general | solution.py:125
  238.0 8.2 %all-to-all-done.10 = bf16[2,256,1024]{2,1,0:T(8,128)(2,1)} async-done(((bf16[2,256,1024]{2,1,0:T(8,128)(2,1)}), bf16[2,256,1024]{2,1,0:T(8,128)(2,1)}, u32[]{:S(2)}, u32[]{:S(2)}) %all-to-all-start.10) | async-done | bytes 1048608 | tf_op jit(solution)/shard_map/all_to_all | solution.py:47
  246.2 2.4 reduce_sum.142
  248.6 4.6 %all-to-all-start.11 = ((bf16[32,8,1024]{2,1,0:T(8,128)(2,1)}), bf16[32,8,1024]{2,1,0:T(8,128)(2,1)}, u32[]{:S(2)}, u32[]{:S(2)}) async-start(bf16[32,8,1024]{2,1,0:T(8,128)(2,1)} %bitcast.147), calls=%async_computation.11 | async-start | bytes 1048576 | tf_op jit(solution)/shard_map/all_to_all | solution.py:39
  253.3 4.5 %convolution_convert_fusion.1 = bf16[2,1024,1024]{2,1,0:T(8,128)(2,1)} fusion(bf16[256,2,1024]{2,0,1:T(8,128)(2,1)S(1)} %bitcast.142, bf16[256,2,1024]{2,0,1:T(8,128)(2,1)} %copy-done.11), kind=kOutput, calls=%fused_computation.5 | convolution fusion | flops 1075838976 | bytes 6291456 | tf_op jit(solution)/shard_map/gjd,gjf->jdf/dot_general | solution.py:128
  258.8 6.4 %all-to-all-done.11 = bf16[32,8,1024]{2,1,0:T(8,128)(2,1)} async-done(((bf16[32,8,1024]{2,1,0:T(8,128)(2,1)}), bf16[32,8,1024]{2,1,0:T(8,128)(2,1)}, u32[]{:S(2)}, u32[]{:S(2)}) %all-to-all-start.11) | async-done | bytes 524320 | tf_op jit(solution)/shard_map/all_to_all | solution.py:39
  267.3 4.4 %all-to-all-start.12 = ((bf16[32,8,1024]{2,1,0:T(8,128)(2,1)}), bf16[32,8,1024]{2,1,0:T(8,128)(2,1)S(1)}, u32[]{:S(2)}, u32[]{:S(2)}) async-start(bf16[32,8,1024]{2,1,0:T(8,128)(2,1)} %broadcast_in_dim.17), calls=%async_computation.12 | async-start | bytes 1048576 | tf_op jit(solution)/shard_map/all_to_all | solution.py:16
  271.7 3.9 convolution_convert_fusion.3
  275.5 130.9 %all-reduce.2.cloned.1.call-done = f32[1024,64]{0,1:T(8,128)} async-done(((f32[1024,64]{0,1:T(8,128)}), f32[1024,64]{0,1:T(8,128)}) %all-reduce.2.cloned.1.call-update) | async-done | bytes 262160 | tf_op jit(solution)/shard_map/psum | solution.py:159
  407.5 1.8 subtract_divide_fusion
  (66 shorter events, 30.7 us)
Async XLA Ops:
  7.2 32.5 %copy-start = (bf16[2,256,1024]{2,1,0:T(8,128)(2,1)S(1)}, bf16[2,256,1024]{2,1,0:T(8,128)(2,1)}, u32[]{:S(2)}) copy-start(bf16[2,256,1024]{2,1,0:T(8,128)(2,1)} %param.7) | copy-start | bytes 3145732
  9.9 5.1 %copy-start.6 = (bf16[1024,64]{0,1:T(8,128)(2,1)S(1)}, bf16[1024,64]{0,1:T(8,128)(2,1)}, u32[]{:S(2)}) copy-start(bf16[1024,64]{0,1:T(8,128)(2,1)} %param.11) | copy-start | bytes 393220
  9.9 29.8 %all-to-all-start = ((bf16[4,256,1024]{2,1,0:T(8,128)(2,1)}), bf16[4,256,1024]{2,1,0:T(8,128)(2,1)S(1)}, u32[]{:S(2)}, u32[]{:S(2)}) async-start(bf16[4,256,1024]{2,1,0:T(8,128)(2,1)} %broadcast_in_dim.12), calls=%async_computation | async-start | bytes 4194304 | tf_op jit(solution)/shard_map/all_to_all | solution.py:16
  39.7 1.3 copy-start.7
  48.0 20.2 %all-to-all-start.3 = ((bf16[2,64,1024]{2,0,1:T(2,128)(2,1)}), bf16[2,64,1024]{2,0,1:T(2,128)(2,1)}, u32[]{:S(2)}, u32[]{:S(2)}) async-start(bf16[2,64,1024]{2,0,1:T(2,128)(2,1)} %copy.81), calls=%async_computation.3 | async-start | bytes 524288 | tf_op jit(solution)/shard_map/all_to_all | solution.py:98
  68.2 14.1 %all-to-all-start.1 = ((bf16[2,64,1024]{2,0,1:T(2,128)(2,1)}), bf16[2,64,1024]{2,0,1:T(2,128)(2,1)}, u32[]{:S(2)}, u32[]{:S(2)}) async-start(bf16[2,64,1024]{2,0,1:T(2,128)(2,1)} %copy.77), calls=%async_computation.1 | async-start | bytes 524288 | tf_op jit(solution)/shard_map/all_to_all | solution.py:116
  84.4 21.2 %all-to-all-start.4 = ((bf16[4,64,2,1024]{3,1,2,0:T(8,128)(2,1)}), bf16[4,64,2,1024]{3,1,2,0:T(8,128)(2,1)}, u32[]{:S(2)}, u32[]{:S(2)}) async-start(bf16[4,64,2,1024]{3,1,2,0:T(8,128)(2,1)} %broadcast_in_dim.16), calls=%async_computation.4 | async-start | bytes 2097152 | tf_op jit(solution)/shard_map/all_to_all | solution.py:16
  107.6 18.8 %all-to-all-start.2 = ((bf16[4,64,2,1024]{3,1,2,0:T(8,128)(2,1)}), bf16[4,64,2,1024]{3,1,2,0:T(8,128)(2,1)}, u32[]{:S(2)}, u32[]{:S(2)}) async-start(bf16[4,64,2,1024]{3,1,2,0:T(8,128)(2,1)} %broadcast_in_dim.14), calls=%async_computation.2 | async-start | bytes 2097152 | tf_op jit(solution)/shard_map/all_to_all | solution.py:16
  114.1 1.0 copy-start.1
  126.4 1.9 copy-start.5
  127.9 5.2 %copy-start.9 = (bf16[4,64,2,1024]{3,1,0,2:T(8,128)(2,1)}, bf16[4,64,2,1024]{3,1,0,2:T(8,128)(2,1)S(1)}, u32[]{:S(2)}) copy-start(bf16[4,64,2,1024]{3,1,0,2:T(8,128)(2,1)S(1)} %copy.80) | copy-start | bytes 3145732
  128.3 4.8 %copy-start.4 = (bf16[2,1024,1024]{2,1,0:T(8,128)(2,1)S(1)}, bf16[2,1024,1024]{2,1,0:T(8,128)(2,1)}, u32[]{:S(2)}) copy-start(bf16[2,1024,1024]{2,1,0:T(8,128)(2,1)} %param.12) | copy-start | bytes 12582916
  133.1 1.3 copy-start.11
  135.5 18.7 %all-to-all-start.5 = ((bf16[4,64,2,1024]{3,1,2,0:T(8,128)(2,1)}), bf16[4,64,2,1024]{3,1,2,0:T(8,128)(2,1)}, u32[]{:S(2)}, u32[]{:S(2)}) async-start(bf16[4,64,2,1024]{3,1,2,0:T(8,128)(2,1)} %copy.85), calls=%async_computation.5 | async-start | bytes 2097152 | tf_op jit(solution)/shard_map/all_to_all | solution.py:39
  154.2 18.8 %all-to-all-start.7 = ((bf16[4,64,2,1024]{3,1,2,0:T(8,128)(2,1)}), bf16[4,64,2,1024]{3,1,2,0:T(8,128)(2,1)}, u32[]{:S(2)}, u32[]{:S(2)}) async-start(bf16[4,64,2,1024]{3,1,2,0:T(8,128)(2,1)} %copy.89), calls=%async_computation.7 | async-start | bytes 2097152 | tf_op jit(solution)/shard_map/all_to_all | solution.py:39
  173.0 14.2 %all-to-all-start.6 = ((bf16[64,2,1024]{2,1,0:T(2,128)(2,1)}), bf16[64,2,1024]{2,1,0:T(2,128)(2,1)}, u32[]{:S(2)}, u32[]{:S(2)}) async-start(bf16[64,2,1024]{2,1,0:T(2,128)(2,1)} %copy.87), calls=%async_computation.6 | async-start | bytes 524288 | tf_op jit(solution)/shard_map/all_to_all | solution.py:139
  187.2 14.1 %all-to-all-start.8 = ((bf16[64,2,1024]{2,1,0:T(2,128)(2,1)}), bf16[64,2,1024]{2,1,0:T(2,128)(2,1)}, u32[]{:S(2)}, u32[]{:S(2)}) async-start(bf16[64,2,1024]{2,1,0:T(2,128)(2,1)} %copy.91), calls=%async_computation.8 | async-start | bytes 524288 | tf_op jit(solution)/shard_map/all_to_all | solution.py:110
  204.9 2.5 copy-start.8
  211.1 2.4 copy-start.3
  214.2 1.3 copy-start.12
  225.0 7.8 %copy-start.10 = (bf16[4,64,2,1024]{3,1,0,2:T(8,128)(2,1)S(1)}, bf16[4,64,2,1024]{3,1,0,2:T(8,128)(2,1)}, u32[]{:S(2)}) copy-start(bf16[4,64,2,1024]{3,1,0,2:T(8,128)(2,1)} %copy-done.9) | copy-start | bytes 3145732
  228.4 17.8 %all-to-all-start.10 = ((bf16[2,256,1024]{2,1,0:T(8,128)(2,1)}), bf16[2,256,1024]{2,1,0:T(8,128)(2,1)}, u32[]{:S(2)}, u32[]{:S(2)}) async-start(bf16[2,256,1024]{2,1,0:T(8,128)(2,1)} %reduce_sum.141), calls=%async_computation.10 | async-start | bytes 2097152 | tf_op jit(solution)/shard_map/all_to_all | solution.py:47
  238.0 15.3 %copy-start.2 = (bf16[4,64,2,1024]{3,1,0,2:T(8,128)(2,1)S(1)}, bf16[4,64,2,1024]{3,1,0,2:T(8,128)(2,1)}, u32[]{:S(2)}) copy-start(bf16[4,64,2,1024]{3,1,0,2:T(8,128)(2,1)} %copy-done.1) | copy-start | bytes 3145732
  248.6 16.7 %all-to-all-start.11 = ((bf16[32,8,1024]{2,1,0:T(8,128)(2,1)}), bf16[32,8,1024]{2,1,0:T(8,128)(2,1)}, u32[]{:S(2)}, u32[]{:S(2)}) async-start(bf16[32,8,1024]{2,1,0:T(8,128)(2,1)} %bitcast.147), calls=%async_computation.11 | async-start | bytes 1048576 | tf_op jit(solution)/shard_map/all_to_all | solution.py:39
  253.2 153.1 %all-reduce.2.cloned.1.call-start = ((), (), s32[]{:S(2)}) async-start(), calls=%async_computation.13 | async-start | bytes 524288 | tf_op jit(solution)/shard_map/psum | solution.py:159
  257.8 13.8 %copy-start.13 = (bf16[512,1024]{1,0:T(8,128)(2,1)S(1)}, bf16[512,1024]{1,0:T(8,128)(2,1)}, u32[]{:S(2)}) copy-start(bf16[512,1024]{1,0:T(8,128)(2,1)} %copy-done.12) | copy-start | bytes 3145732
  267.3 142.0 %all-to-all-start.12 = ((bf16[32,8,1024]{2,1,0:T(8,128)(2,1)}), bf16[32,8,1024]{2,1,0:T(8,128)(2,1)S(1)}, u32[]{:S(2)}, u32[]{:S(2)}) async-start(bf16[32,8,1024]{2,1,0:T(8,128)(2,1)} %broadcast_in_dim.17), calls=%async_computation.12 | async-start | bytes 1048576 | tf_op jit(solution)/shard_map/all_to_all | solution.py:16
Sparse Core Ops, SparseCore 0:
  259.3 146.9 all-reduce.1
where the time goes:
time: 419 us; the launch traced here: 417 us
  waiting for transfers between devices  232 us (55%)
  starting transfers between devices  66.1 us (16%)
  matrix products  44.4 us (11%)
  local copies, waits for them, and re-layouts  33.2 us (8%)
  other arithmetic  17.8 us (4%)
  between operations  14.3 us (3%)
  blocking collectives  9.33 us (2%)
    psum x1, waiting for transfers between devices, shards(): grad_unit = lax.psum(local_unit, IMG_EXP)  131 us
    all_to_all x4, waiting for transfers between devices, copy_for_each(): lax.all_to_all(jnp.broadcast_to(shard[None], (devices, *shard.shape)), ax...  42.7 us
    all_to_all x3, waiting for transfers between devices, summed_on_arrival(): lax.all_to_all(split_up(shard, dim, devices), axis, 0, 0, tiled=True)  24.1 us
    all_to_all x4, starting transfers between devices, copy_for_each(): lax.all_to_all(jnp.broadcast_to(shard[None], (devices, *shard.shape)), ax...  22.3 us
    all_to_all x3, starting transfers between devices, summed_on_arrival(): lax.all_to_all(split_up(shard, dim, devices), axis, 0, 0, tiled=True)  15 us
    all_to_all x1, starting transfers between devices, shards(): lax.all_to_all(slot_in, 'exp', split_axis=1, concat_axis=0, tiled=True)  10.6 us
    all_to_all x1, blocking collectives, summed_on_arrival(): lax.all_to_all(split_up(shard, dim, devices), axis, 0, 0, tiled=True)  9.33 us
    broadcast_in_dim x6, local copies, waits for them, and re-layouts, copy_for_each(): jnp.broadcast_to(shard[None], (devices, *shard.shape))  9.18 us
  transfers between devices with their start and end apart: 13, of which 12 were waited for; matrix products, arithmetic and copies ran while one was open for 11% of the time, Pallas kernels for 0%

commit v1 on v0

--- a/solution.py
+++ b/solution.py
@@ -1,3 +1,4 @@
+import functools
 import math
 import jax
 import jax.numpy as jnp
@@ -9,6 +10,15 @@
 IMG_EXP = ("img_0", "img_1", "exp")
 logit_scale = 48.0
 epsilon = 1e-06
+
+
+def _tell_packet(panel, axis_name, mesh_name):
+    for ix in (axis_name, mesh_name):
+        panel = lax.psum(panel, ix)
+    return panel
+
+
+_enter_quotas = functools.partial(_tell_packet, axis_name="img_0", mesh_name=("img_1", "exp"))
 
 
 def copy_for_each(shard, axis):
@@ -156,7 +166,7 @@
         grad_logits, unit.T, preferred_element_type=jnp.float32
     )
     local_unit = factor * jnp.dot(normed.T, grad_logits, preferred_element_type=jnp.float32)
-    grad_unit = lax.psum(local_unit, IMG_EXP)
+    grad_unit = _enter_quotas(local_unit)
     grad_slots = (
         grad_unit - unit32 * jnp.sum(unit32 * grad_unit, axis=0, keepdims=True)
     ) / slot_norm

time: 419 us -> 923 us (2.20)
  waiting for transfers between devices: 232 us -> 726 us
    psum x1 -> x2, waiting for transfers between devices: 131 us -> 631 us  [_tell_packet(): panel = lax.psum(panel, ix)]
  transfers between devices with their start and end apart: 13 -> 14, of which waited for: 12 -> 12; matrix products, arithmetic and copies ran while one was open for 11% -> 5% of each run, Pallas kernels for 0% -> 0%
where the time goes in v1:
time: 923 us; the launch traced here: 916 us
  waiting for transfers between devices  726 us (79%)
  starting transfers between devices  70.9 us (8%)
  matrix products  44.4 us (5%)
  local copies, waits for them, and re-layouts  33.2 us (4%)
  other arithmetic  17.8 us (2%)
  between operations  14.4 us (2%)
  blocking collectives  9.33 us (1%)
    psum x2, waiting for transfers between devices, _tell_packet(): panel = lax.psum(panel, ix)  631 us
    all_to_all x4, waiting for transfers between devices, copy_for_each(): lax.all_to_all(jnp.broadcast_to(shard[None], (devices, *shard.shape)), ax...  42.7 us
    all_to_all x4, starting transfers between devices, copy_for_each(): lax.all_to_all(jnp.broadcast_to(shard[None], (devices, *shard.shape)), ax...  27 us
  transfers between devices with their start and end apart: 14, of which 12 were waited for; matrix products, arithmetic and copies ran while one was open for 5% of the time, Pallas kernels for 0%

profile of v1, /device:TPU:1, one launch (start us, length us, event | category | flops | bytes accessed | tf_op | source)
XLA Modules:
  0.0 916.1 jit_solution(12971053558434021588)
XLA Ops:
  7.2 2.7 broadcast_in_dim.12
  9.9 5.1 all-to-all-start
  15.1 24.5 %all-to-all-done = bf16[4,256,1024]{2,1,0:T(8,128)(2,1)S(1)} async-done(((bf16[4,256,1024]{2,1,0:T(8,128)(2,1)}), bf16[4,256,1024]{2,1,0:T(8,128)(2,1)S(1)}, u32[]{:S(2)}, u32[]{:S(2)}) %all-to-all-start) | async-done | bytes 2097184 | tf_op jit(solution)/shard_map/all_to_all | solution.py:26
  41.0 3.2 fusion.10
  48.0 10.6 %all-to-all-start.3 = ((bf16[2,64,1024]{2,0,1:T(2,128)(2,1)}), bf16[2,64,1024]{2,0,1:T(2,128)(2,1)}, u32[]{:S(2)}, u32[]{:S(2)}) async-start(bf16[2,64,1024]{2,0,1:T(2,128)(2,1)} %copy.81), calls=%async_computation.3 | async-start | bytes 524288 | tf_op jit(solution)/shard_map/all_to_all | solution.py:108
  61.2 7.1 all-to-all-done.3
  68.2 4.6 all-to-all-start.1
  74.7 7.6 all-to-all-done.1
  82.3 2.0 broadcast_in_dim.16
  84.4 7.7 all-to-all-start.4
  93.9 11.7 %all-to-all-done.4 = bf16[4,64,2,1024]{3,1,2,0:T(8,128)(2,1)} async-done(((bf16[4,64,2,1024]{3,1,2,0:T(8,128)(2,1)}), bf16[4,64,2,1024]{3,1,2,0:T(8,128)(2,1)}, u32[]{:S(2)}, u32[]{:S(2)}) %all-to-all-start.4) | async-done | bytes 1048608 | tf_op jit(solution)/shard_map/all_to_all | solution.py:26
  105.6 2.0 broadcast_in_dim.14
  107.6 5.2 all-to-all-start.2
  115.1 4.8 fusion.45
  119.9 6.5 all-to-all-done.2
  128.3 4.7 fusion.17
  135.5 5.2 all-to-all-start.5
  140.6 4.2 convolution_convert_fusion.4
  146.0 8.2 all-to-all-done.5
  154.2 5.2 all-to-all-start.7
  159.4 2.2 reduce_sum.136
  161.6 1.9 copy.87
  163.5 9.5 %all-to-all-done.7 = bf16[4,64,2,1024]{3,1,2,0:T(8,128)(2,1)} async-done(((bf16[4,64,2,1024]{3,1,2,0:T(8,128)(2,1)}), bf16[4,64,2,1024]{3,1,2,0:T(8,128)(2,1)}, u32[]{:S(2)}, u32[]{:S(2)}) %all-to-all-start.7) | async-done | bytes 1048608 | tf_op jit(solution)/shard_map/all_to_all | solution.py:49
  173.0 4.6 all-to-all-start.6
  177.6 2.2 reduce_sum.137
  179.8 1.9 copy.91
  181.7 5.5 all-to-all-done.6
  187.2 4.6 all-to-all-start.8
  191.8 1.8 copy.88
  195.4 5.9 all-to-all-done.8
  201.3 1.8 copy.92
  204.9 1.8 convolution_bitcast_fusion
  207.4 1.9 fusion.37
  209.2 1.9 fusion.30
  211.1 2.4 fusion.5
  215.7 9.3 %all_to_all.112 = bf16[2,2,256,1024]{3,2,1,0:T(8,128)(2,1)} all-to-all(bf16[2,2,256,1024]{3,2,1,0:T(8,128)(2,1)S(1)} %bitcast.143), channel_id=1, replica_groups=mesh['img_0'=2,'img_1'=2,'exp'=32] {'img_1'}, dimensions={0} | all-to-all | bytes 4194304 | tf_op jit(solution)/shard_map/all_to_all | solution.py:49
  225.0 3.4 reduce_sum.141
  228.4 4.4 all-to-all-start.10
  232.8 5.1 convolution_convert_fusion
  238.0 8.2 all-to-all-done.10
  246.2 2.4 reduce_sum.142
  248.6 4.6 all-to-all-start.11
  254.4 4.5 convolution_convert_fusion.1
  258.9 29.5 %all-reduce.3.cloned.1.call-done = f32[1024,64]{0,1:T(8,128)} async-done(((f32[1024,64]{0,1:T(8,128)}), f32[1024,64]{0,1:T(8,128)}) %all-reduce.3.cloned.1.call-update) | async-done | bytes 262160 | tf_op jit(solution)/shard_map/psum | solution.py:17
  290.5 9.1 all-to-all-start.12
  299.6 3.8 convolution_convert_fusion.3
  303.4 601.8 %all-reduce.5.cloned.1.call-done = f32[1024,64]{0,1:T(8,128)} async-done(((f32[1024,64]{0,1:T(8,128)}), f32[1024,64]{0,1:T(8,128)}) %all-reduce.5.cloned.1.call-update) | async-done | bytes 262160 | tf_op jit(solution)/shard_map/psum | solution.py:17
  906.4 1.8 subtract_divide_fusion
  (69 shorter events, 30.8 us)
Async XLA Ops:
  7.2 32.5 %copy-start = (bf16[2,256,1024]{2,1,0:T(8,128)(2,1)S(1)}, bf16[2,256,1024]{2,1,0:T(8,128)(2,1)}, u32[]{:S(2)}) copy-start(bf16[2,256,1024]{2,1,0:T(8,128)(2,1)} %param.7) | copy-start | bytes 3145732
  9.9 5.1 copy-start.6
  9.9 29.8 %all-to-all-start = ((bf16[4,256,1024]{2,1,0:T(8,128)(2,1)}), bf16[4,256,1024]{2,1,0:T(8,128)(2,1)S(1)}, u32[]{:S(2)}, u32[]{:S(2)}) async-start(bf16[4,256,1024]{2,1,0:T(8,128)(2,1)} %broadcast_in_dim.12), calls=%async_computation | async-start | bytes 4194304 | tf_op jit(solution)/shard_map/all_to_all | solution.py:26
  39.7 1.3 copy-start.7
  48.0 20.2 %all-to-all-start.3 = ((bf16[2,64,1024]{2,0,1:T(2,128)(2,1)}), bf16[2,64,1024]{2,0,1:T(2,128)(2,1)}, u32[]{:S(2)}, u32[]{:S(2)}) async-start(bf16[2,64,1024]{2,0,1:T(2,128)(2,1)} %copy.81), calls=%async_computation.3 | async-start | bytes 524288 | tf_op jit(solution)/shard_map/all_to_all | solution.py:108
  68.2 14.1 %all-to-all-start.1 = ((bf16[2,64,1024]{2,0,1:T(2,128)(2,1)}), bf16[2,64,1024]{2,0,1:T(2,128)(2,1)}, u32[]{:S(2)}, u32[]{:S(2)}) async-start(bf16[2,64,1024]{2,0,1:T(2,128)(2,1)} %copy.77), calls=%async_computation.1 | async-start | bytes 524288 | tf_op jit(solution)/shard_map/all_to_all | solution.py:126
  84.4 21.2 %all-to-all-start.4 = ((bf16[4,64,2,1024]{3,1,2,0:T(8,128)(2,1)}), bf16[4,64,2,1024]{3,1,2,0:T(8,128)(2,1)}, u32[]{:S(2)}, u32[]{:S(2)}) async-start(bf16[4,64,2,1024]{3,1,2,0:T(8,128)(2,1)} %broadcast_in_dim.16), calls=%async_computation.4 | async-start | bytes 2097152 | tf_op jit(solution)/shard_map/all_to_all | solution.py:26
  107.6 18.8 %all-to-all-start.2 = ((bf16[4,64,2,1024]{3,1,2,0:T(8,128)(2,1)}), bf16[4,64,2,1024]{3,1,2,0:T(8,128)(2,1)}, u32[]{:S(2)}, u32[]{:S(2)}) async-start(bf16[4,64,2,1024]{3,1,2,0:T(8,128)(2,1)} %broadcast_in_dim.14), calls=%async_computation.2 | async-start | bytes 2097152 | tf_op jit(solution)/shard_map/all_to_all | solution.py:26
  114.1 1.0 copy-start.1
  126.4 1.9 copy-start.5
  127.9 5.2 copy-start.9
  128.3 4.8 copy-start.4
  133.1 1.3 copy-start.11
  135.5 18.7 %all-to-all-start.5 = ((bf16[4,64,2,1024]{3,1,2,0:T(8,128)(2,1)}), bf16[4,64,2,1024]{3,1,2,0:T(8,128)(2,1)}, u32[]{:S(2)}, u32[]{:S(2)}) async-start(bf16[4,64,2,1024]{3,1,2,0:T(8,128)(2,1)} %copy.85), calls=%async_computation.5 | async-start | bytes 2097152 | tf_op jit(solution)/shard_map/all_to_all | solution.py:49
  154.2 18.8 %all-to-all-start.7 = ((bf16[4,64,2,1024]{3,1,2,0:T(8,128)(2,1)}), bf16[4,64,2,1024]{3,1,2,0:T(8,128)(2,1)}, u32[]{:S(2)}, u32[]{:S(2)}) async-start(bf16[4,64,2,1024]{3,1,2,0:T(8,128)(2,1)} %copy.89), calls=%async_computation.7 | async-start | bytes 2097152 | tf_op jit(solution)/shard_map/all_to_all | solution.py:49
  173.0 14.2 %all-to-all-start.6 = ((bf16[64,2,1024]{2,1,0:T(2,128)(2,1)}), bf16[64,2,1024]{2,1,0:T(2,128)(2,1)}, u32[]{:S(2)}, u32[]{:S(2)}) async-start(bf16[64,2,1024]{2,1,0:T(2,128)(2,1)} %copy.87), calls=%async_computation.6 | async-start | bytes 524288 | tf_op jit(solution)/shard_map/all_to_all | solution.py:149
  187.2 14.1 %all-to-all-start.8 = ((bf16[64,2,1024]{2,1,0:T(2,128)(2,1)}), bf16[64,2,1024]{2,1,0:T(2,128)(2,1)}, u32[]{:S(2)}, u32[]{:S(2)}) async-start(bf16[64,2,1024]{2,1,0:T(2,128)(2,1)} %copy.91), calls=%async_computation.8 | async-start | bytes 524288 | tf_op jit(solution)/shard_map/all_to_all | solution.py:120
  204.9 2.5 copy-start.8
  211.1 2.4 copy-start.3
  214.2 1.3 copy-start.12
  225.0 7.8 copy-start.10
  228.4 17.8 %all-to-all-start.10 = ((bf16[2,256,1024]{2,1,0:T(8,128)(2,1)}), bf16[2,256,1024]{2,1,0:T(8,128)(2,1)}, u32[]{:S(2)}, u32[]{:S(2)}) async-start(bf16[2,256,1024]{2,1,0:T(8,128)(2,1)} %reduce_sum.141), calls=%async_computation.10 | async-start | bytes 2097152 | tf_op jit(solution)/shard_map/all_to_all | solution.py:57
  238.0 16.4 %copy-start.2 = (bf16[4,64,2,1024]{3,1,0,2:T(8,128)(2,1)S(1)}, bf16[4,64,2,1024]{3,1,0,2:T(8,128)(2,1)}, u32[]{:S(2)}) copy-start(bf16[4,64,2,1024]{3,1,0,2:T(8,128)(2,1)} %copy-done.1) | copy-start | bytes 3145732
  248.6 39.9 %all-to-all-start.11 = ((bf16[32,8,1024]{2,1,0:T(8,128)(2,1)}), bf16[32,8,1024]{2,1,0:T(8,128)(2,1)}, u32[]{:S(2)}, u32[]{:S(2)}) async-start(bf16[32,8,1024]{2,1,0:T(8,128)(2,1)} %bitcast.147), calls=%async_computation.11 | async-start | bytes 1048576 | tf_op jit(solution)/shard_map/all_to_all | solution.py:49
  253.2 35.2 %all-reduce.3.cloned.1.call-start = ((), (), s32[]{:S(2)}) async-start(), calls=%async_computation.13 | async-start | bytes 524288 | tf_op jit(solution)/shard_map/psum | solution.py:17
  254.3 651.0 %all-reduce.5.cloned.1.call-start = ((), (), s32[]{:S(2)}) async-start(), calls=%async_computation.14 | async-start | bytes 524288 | tf_op jit(solution)/shard_map/psum | solution.py:17
  258.9 40.7 %copy-start.13 = (bf16[512,1024]{1,0:T(8,128)(2,1)S(1)}, bf16[512,1024]{1,0:T(8,128)(2,1)}, u32[]{:S(2)}) copy-start(bf16[512,1024]{1,0:T(8,128)(2,1)} %copy-done.12) | copy-start | bytes 3145732
  290.5 617.7 %all-to-all-start.12 = ((bf16[32,8,1024]{2,1,0:T(8,128)(2,1)}), bf16[32,8,1024]{2,1,0:T(8,128)(2,1)S(1)}, u32[]{:S(2)}, u32[]{:S(2)}) async-start(bf16[32,8,1024]{2,1,0:T(8,128)(2,1)} %broadcast_in_dim.17), calls=%async_computation.12 | async-start | bytes 1048576 | tf_op jit(solution)/shard_map/all_to_all | solution.py:26
Sparse Core Ops, SparseCore 0:
  257.0 31.3 all-reduce.2
  290.9 614.2 all-reduce.4
